TPU v7x, 256 devices: a whole 4x4x8 slice. The times are simulated.
256 devices in a mesh: ctx: 32 (over x, z), head: 8 (over y, core).
Axes of the slice: x: 4, y: 4, z: 8, core: 2. Of those that a mesh axis runs over, the one named last changes fastest.
Arguments:
- queries: bfloat16 [8192, 32, 128], P('ctx', 'head'), may hold values from -40 to 40
- keys: bfloat16 [8192, 8, 128], P('ctx', 'head'), may hold values from -40 to 40
- values: bfloat16 [8192, 8, 128], P('ctx', 'head'), may hold values from -6 to 6
- doc_ids: int32 [8192], P('ctx'), may hold values from 0 to 3, never falling along the last dimension, each value on 1 to 4096 neighbouring positions
Outputs:
- attended: bfloat16 [8192, 4096], P(('ctx', 'head'))
Inputs may be any that keep to these rules, and one draw needn't show every extreme that they name: `doc_ids`: document numbers never fall along the sequence; each document has 1 to 4096 tokens and one has exactly 4096.
All inputs are finite; a program needn't handle non-finite values.
Results may differ from a plain program's by a relative error of at most 0.009.
Values may be sent and summed in bfloat16 or wider, within the bound.
No kernel may reach another device: no remote copies, remote signals or barrier semaphores. Data moves between devices by JAX's collectives and lax.ppermute only.
A program may use at most 128 MiB of HBM per device.

v0:
```python
import jax
import jax.numpy as jnp
from jax import lax
from jax.sharding import PartitionSpec as P


def attend(query_sets, keys, values, all_ids):
    kv_heads = keys.shape[1]
    head_dim = keys.shape[2]
    score_scale = head_dim ** (-0.5)
    prepared = []
    initial = []
    for query_rows, query_start in query_sets:
        row_count = query_rows.shape[0]
        q_heads = query_rows.shape[1]
        group_size = q_heads // kv_heads
        grouped = query_rows.reshape(row_count, kv_heads, group_size, head_dim)
        query_pos = query_start + jnp.arange(row_count, dtype=jnp.int32)
        query_ids = lax.dynamic_slice_in_dim(all_ids, query_start, row_count, 0)
        last_pos = query_start + row_count - 1
        prepared.append((grouped, query_pos, query_ids, last_pos))
        initial.append(
            (
                jnp.full((kv_heads, group_size, row_count), -1e30, jnp.float32),
                jnp.zeros((kv_heads, group_size, row_count), jnp.float32),
                jnp.zeros((kv_heads, group_size, row_count, head_dim), jnp.float32),
            )
        )
    carried = tuple(initial)
    key_start = jnp.int32(0)
    key_piece = lax.all_gather(keys, "ctx", axis=0, tiled=True)
    value_piece = lax.all_gather(values, "ctx", axis=0, tiled=True)
    piece_len = key_piece.shape[0]
    key_pos = jnp.arange(piece_len, dtype=jnp.int32)
    updated = []
    for (grouped, query_pos, query_ids, last_pos), state_now in zip(prepared, carried):

        def update(state_old, grouped=grouped, query_pos=query_pos, query_ids=query_ids):
            old_max, old_sum, accumulated = state_old
            scores = (
                jnp.einsum("nhgd,khd->hgnk", grouped, key_piece, preferred_element_type=jnp.float32)
                * score_scale
            )
            visible = (key_pos[None, :] <= query_pos[:, None]) & (
                all_ids[None, :] == query_ids[:, None]
            )
            scores = jnp.where(visible, scores, jnp.float32(-1e30))
            new_max = jnp.maximum(old_max, jnp.max(scores, axis=-1))
            weights = jnp.where(visible, jnp.exp(scores - new_max[..., None]), jnp.float32(0.0))
            new_sum = jnp.sum(weights, axis=-1)
            product = jnp.einsum(
                "hgnk,khd->hgnd",
                weights.astype(jnp.bfloat16),
                value_piece,
                preferred_element_type=jnp.float32,
            )
            return (new_max, new_sum, product)

        def unchanged(state_old):
            return state_old

        updated.append(lax.cond(key_start <= last_pos, update, unchanged, state_now))
    finals = tuple(updated)
    outputs = []
    for final_state in finals:
        run_max, run_sum, accumulated = final_state
        normed = accumulated / run_sum[..., None]
        row_count = normed.shape[2]
        joined = jnp.transpose(normed, (2, 0, 1, 3)).reshape(row_count, -1)
        outputs.append(joined.astype(jnp.bfloat16))
    return outputs


def local(queries, keys, values, doc_ids):
    tok_rows = queries.shape[0]
    ctx_place = lax.axis_index("ctx")
    all_ids = lax.all_gather(doc_ids, "ctx", axis=0, tiled=True)
    results = attend([(queries, ctx_place * tok_rows)], keys, values, all_ids)
    merged = results[0]
    return lax.all_to_all(merged, "head", split_axis=0, concat_axis=1, tiled=True)


def solution(mesh):
    return jax.shard_map(
        local,
        mesh=mesh,
        in_specs=(P("ctx", "head", None), P("ctx", "head", None), P("ctx", "head", None), P("ctx")),
        out_specs=P(("ctx", "head"), None),
        check_vma=False,
    )
```

profile of v0, /device:TPU:1, one launch (start us, length us, event | category | flops | bytes accessed | tf_op | source)
XLA Modules:
  0.0 239.5 jit_solution(13473183504084923722)
XLA Ops:
  6.5 0.0 all-gather.4.cloned.1.call-start
  6.5 0.7 all-gather.4.cloned.1.call-update
  7.3 0.0 all-gather.6.cloned.1.call-start
  7.3 0.7 all-gather.6.cloned.1.call-update
  8.0 37.9 %all-gather = s32[32,1,256]{2,1,0:T(1,128)S(1)} all-gather(s32[1,1,256]{2,1,0:T(1,128)} %bitcast.51), channel_id=1, replica_groups=mesh['ctx'=32,'head'=8] {'ctx'}, dimensions={0}, use_global_device_ids=true | all-gather | bytes 33792 | tf_op jit(solution)/shard_map/all_gather | solution.py:77
  46.0 41.1 %all-gather.4.cloned.1.call-done = bf16[8192,1,128]{2,0,1:T(8,128)(2,1)} async-done(((bf16[256,1,128]{2,0,1:T(8,128)(2,1)}), bf16[8192,1,128]{2,0,1:T(8,128)(2,1)}) %all-gather.4.cloned.1.call-update) | async-done | bytes 2097168 | tf_op jit(solution)/shard_map/all_gather | solution.py:31
  87.0 77.7 %all-gather.6.cloned.1.call-done = bf16[8192,1,128]{2,0,1:T(8,128)(2,1)} async-done(((bf16[256,1,128]{2,0,1:T(8,128)(2,1)}), bf16[8192,1,128]{2,0,1:T(8,128)(2,1)}) %all-gather.6.cloned.1.call-update) | async-done | bytes 2097168 | tf_op jit(solution)/shard_map/all_gather | solution.py:32
  164.7 50.8 %conditional.1 = (f32[1,4,256]{2,1,0:T(4,128)S(1)}, f32[1,4,256,128]{3,2,1,0:T(8,128)S(1)}) conditional(s32[]{:T(128)} %convert_element_type.17, () %tuple.16, (s32[8192]{0:T(1024)S(1)}, s32[]{:T(128)}, s32[256]{0:T(256)S(1)}, s32[8192]{0:T(1024)S(1)}, bf16[8192,1,128]{2,0,1:T(8,128)(2,1)}, /*index=5*/bf16[256,4,128]{2,1,0:T(4,128)(2,1)}, ...), branch_computations={%region_0.0_spmd, %region_1.4_spmd} | conditional | flops 4410309632 | bytes 122517592 | solution.py:62
  164.7 0.0 copy-start
  164.8 0.1 dynamic_slice.4
  164.8 5.6 %compare_and_fusion = pred[256,8192]{0,1:T(8,128)(4,1)S(1)} fusion(s32[256]{0:T(256)S(1)} %dynamic_slice.4, s32[256]{0:T(256)S(1)} %broadcast_add_fusion, s32[8192]{0:T(1024)S(1)} %get-tuple-element.58, s32[8192]{0:T(1024)S(1)} %get-tuple-element.55), kind=kLoop, calls=%fused_computation.8 | loop fusion | flops 6291456 | bytes 2164736 | tf_op jit(solution)/shard_map/cond/branch_1_fun/and | solution.py:44
  170.5 14.7 %fusion = (f32[4,256]{1,0:T(4,128)S(1)}, f32[8192,256,4]{1,0,2:T(8,128)}) fusion(pred[256,8192]{0,1:T(8,128)(4,1)S(1)} %compare_and_fusion, bf16[256,4,128]{2,1,0:T(4,128)(2,1)} %get-tuple-element.94, bf16[8192,1,128]{2,0,1:T(8,128)(2,1)} %get-tuple-element.59), kind=kOutput, calls=%fused_computation.2 | convolution fusion | flops 2172648448 | bytes 38014976 | tf_op jit(solution)/shard_map/cond/branch_1_fun/nhgd,khd->hgnk/dot_general | solution.py:41
  185.2 0.0 copy-done
  185.2 15.2 %fusion.10 = f32[1,4,256,128]{3,2,1,0:T(8,128)S(1)} fusion(bf16[8192,1,128]{2,0,1:T(8,128)(2,1)S(1)} %copy-done, f32[8192,256,4]{1,0,2:T(8,128)} %get-tuple-element.97, f32[4,256]{1,0:T(4,128)S(1)} %broadcast_maximum_fusion, pred[256,8192]{0,1:T(8,128)(4,1)S(1)} %compare_and_fusion), kind=kOutput, calls=%fused_computation.12 | convolution fusion | flops 2189426688 | bytes 38277120 | tf_op jit(solution)/shard_map/cond/branch_1_fun/hgnk,khd->hgnd/dot_general | solution.py:51
  200.5 15.0 %fusion.2 = f32[4,256]{1,0:T(4,128)S(1)} fusion(f32[8192,256,4]{1,0,2:T(8,128)} %get-tuple-element.97, f32[4,256]{1,0:T(4,128)S(1)} %broadcast_maximum_fusion, pred[256,8192]{0,1:T(8,128)(4,1)S(1)} %compare_and_fusion), kind=kLoop, calls=%fused_computation.4 | loop fusion | flops 41942016 | bytes 35659776 | tf_op jit(solution)/shard_map/cond/branch_1_fun/reduce_sum | solution.py:50
  215.5 0.2 fusion.19
  215.7 0.2 copy.17
  215.9 0.1 convert_element_type.20
  216.0 15.9 %all_to_all.16 = bf16[8,32,512]{2,1,0:T(8,128)(2,1)S(1)} all-to-all(bf16[8,32,512]{2,1,0:T(8,128)(2,1)S(1)} %convert_element_type.20), channel_id=1, replica_groups=mesh['ctx'=32,'head'=8] {'head'}, dimensions={0} | all-to-all | bytes 524288 | tf_op jit(solution)/shard_map/all_to_all | solution.py:80
  231.9 0.7 copy.20
  (4 shorter events, 0.0 us)
Async XLA Ops:
  6.5 80.5 %all-gather.4.cloned.1.call-start = ((), (), s32[]{:S(2)}) async-start(), calls=%async_computation.1 | async-start | bytes 2162688 | tf_op jit(solution)/shard_map/all_gather | solution.py:31
  7.3 157.5 %all-gather.6.cloned.1.call-start = ((), (), s32[]{:S(2)}) async-start(), calls=%async_computation.2 | async-start | bytes 2162688 | tf_op jit(solution)/shard_map/all_gather | solution.py:32
  164.7 20.5 %copy-start = (bf16[8192,1,128]{2,0,1:T(8,128)(2,1)S(1)}, bf16[8192,1,128]{2,0,1:T(8,128)(2,1)}, u32[]{:S(2)}) copy-start(bf16[8192,1,128]{2,0,1:T(8,128)(2,1)} %get-tuple-element.61) | copy-start | bytes 6291460 | tf_op jit(solution)/shard_map/cond
Sparse Core Ops, SparseCore 0:
  9.9 77.0 all-gather.3
  89.6 75.0 all-gather.5
where the time goes:
time: 240 us; the launch traced here: 239 us
  waiting for transfers between devices  120 us (50%)
  blocking collectives  53.8 us (22%)
  matrix products  30 us (12%)
  other arithmetic  20.9 us (9%)
  between operations  13.4 us (6%)
    all_gather x1, waiting for transfers between devices, attend(): value_piece = lax.all_gather(values, 'ctx', axis=0, tiled=True)  77.7 us
    all_gather x1, waiting for transfers between devices, attend(): key_piece = lax.all_gather(keys, 'ctx', axis=0, tiled=True)  41.1 us
    all_gather x1, blocking collectives, local(): all_ids = lax.all_gather(doc_ids, 'ctx', axis=0, tiled=True)  37.9 us
    all_to_all x1, blocking collectives, local(): lax.all_to_all(merged, 'head', split_axis=0, concat_axis=1, tiled=True)  15.9 us
    dot_general x1, matrix products, update(): jnp.einsum('hgnk,khd->hgnd', weights.astype(jnp.bfloat16), value_piece, p...  15.2 us
    reduce_sum x1, other arithmetic, update(): new_sum = jnp.sum(weights, axis=-1)  15 us
    dot_general x1, matrix products, update(): jnp.einsum('nhgd,khd->hgnk', grouped, key_piece, preferred_element_type=j...  14.7 us
    and x1, other arithmetic, update(): (key_pos[None, :] <= query_pos[:, None]) & (all_ids[None, :] == query_ids...  5.61 us
  transfers between devices with their start and end apart: 2, of which 2 were waited for; matrix products, arithmetic and copies ran while one was open for 0% of the time, Pallas kernels for 0%

commit v1 on v0

--- a/solution.py
+++ b/solution.py
@@ -29,7 +29,11 @@
     carried = tuple(initial)
     key_start = jnp.int32(0)
     key_piece = lax.all_gather(keys, "ctx", axis=0, tiled=True)
-    value_piece = lax.all_gather(values, "ctx", axis=0, tiled=True)
+    tables_wrap = lambda field_in, lane_axis: jnp.concatenate(
+        lax.all_to_all(jnp.stack([field_in] * lax.psum(1, lane_axis), axis=0), lane_axis, 0, 0),
+        axis=0,
+    )
+    value_piece = tables_wrap(values, "ctx")
     piece_len = key_piece.shape[0]
     key_pos = jnp.arange(piece_len, dtype=jnp.int32)
     updated = []

time: 240 us -> 178 us (0.74)
  waiting for transfers between devices: 120 us -> 0.71 us
  blocking collectives: 53.8 us -> 97.2 us
  starting transfers between devices: 0.04 us -> 11.9 us
  local copies, waits for them, and re-layouts: 1.12 us -> 3.77 us
    all_gather x1 -> x0, waiting for transfers between devices: 77.7 us -> none  [attend(): value_piece = lax.all_gather(values, 'ctx', axis=0, tiled=True)]
    all_gather x1, blocking collectives: 37.9 us -> 79.8 us  [local(): all_ids = lax.all_gather(doc_ids, 'ctx', axis=0, tiled=True)]
    all_gather x1, waiting for transfers between devices: 41.1 us -> 0.01 us  [attend(): key_piece = lax.all_gather(keys, 'ctx', axis=0, tiled=True)]
    all_to_all x0 -> x1, starting transfers between devices: none -> 11.9 us  [attend(): lax.all_to_all(jnp.stack([field_in] * lax.psum(1, lane_axis), axis=0), la...]
    another operation x0 -> x1, local copies, waits for them, and re-layouts: none -> 2.65 us  [attend(): jnp.stack([field_in] * lax.psum(1, lane_axis), axis=0)]
  transfers between devices with their start and end apart: 2 -> 2, of which waited for: 2 -> 0; matrix products, arithmetic and copies ran while one was open for 0% -> 1% of each run, Pallas kernels for 0% -> 0%
where the time goes in v1:
time: 178 us
  blocking collectives  97.2 us (55%)
  matrix products  30 us (17%)
  other arithmetic  20.9 us (12%)
  between operations  13.4 us (8%)
  starting transfers between devices  11.9 us (7%)
  local copies, waits for them, and re-layouts  3.77 us (2%)
    all_gather x1, blocking collectives, local(): all_ids = lax.all_gather(doc_ids, 'ctx', axis=0, tiled=True)  79.8 us
    all_to_all x1, blocking collectives, local(): lax.all_to_all(merged, 'head', split_axis=0, concat_axis=1, tiled=True)  17.4 us
    dot_general x1, matrix products, update(): jnp.einsum('hgnk,khd->hgnd', weights.astype(jnp.bfloat16), value_piece, p...  15.2 us
    reduce_sum x1, other arithmetic, update(): new_sum = jnp.sum(weights, axis=-1)  15 us
    dot_general x1, matrix products, update(): jnp.einsum('nhgd,khd->hgnk', grouped, key_piece, preferred_element_type=j...  14.7 us
    all_to_all x1, starting transfers between devices, attend(): lax.all_to_all(jnp.stack([field_in] * lax.psum(1, lane_axis), axis=0), la...  11.9 us
    and x1, other arithmetic, update(): (key_pos[None, :] <= query_pos[:, None]) & (all_ids[None, :] == query_ids...  5.61 us
  transfers between devices with their start and end apart: 2, of which 0 were waited for; matrix products, arithmetic and copies ran while one was open for 1% of the time, Pallas kernels for 0%

profile of v1, /device:TPU:1, one launch (start us, length us, event | category | flops | bytes accessed | tf_op | source)
XLA Modules:
  0.0 177.8 jit_solution(9789507428989010783)
XLA Ops:
  6.5 0.0 all-gather.3.cloned.1.call-start
  6.5 0.7 all-gather.3.cloned.1.call-update
  7.3 2.6 %stack.2 = bf16[32,256,1,128]{3,1,2,0:T(8,128)(2,1)} broadcast(bf16[256,128]{1,0:T(8,128)(2,1)} %bitcast.51), dimensions={1,3} | broadcast | bytes 2162688 | tf_op jit(solution)/shard_map/stack | solution.py:33
  9.9 11.9 %all-to-all-start = ((bf16[32,256,1,128]{3,1,2,0:T(8,128)(2,1)}), bf16[32,256,1,128]{3,1,2,0:T(8,128)(2,1)S(1)}, u32[]{:S(2)}, u32[]{:S(2)}) async-start(bf16[32,256,1,128]{3,1,2,0:T(8,128)(2,1)} %stack.2), calls=%async_computation | async-start | bytes 4194304 | tf_op jit(solution)/shard_map/all_to_all | solution.py:33
  21.8 79.8 %all-gather = s32[32,1,256]{2,1,0:T(1,128)S(1)} all-gather(s32[1,1,256]{2,1,0:T(1,128)} %bitcast.54), channel_id=1, replica_groups=mesh['ctx'=32,'head'=8] {'ctx'}, dimensions={0}, use_global_device_ids=true | all-gather | bytes 33792 | tf_op jit(solution)/shard_map/all_gather | solution.py:81
  101.6 0.0 all-gather.3.cloned.1.call-done
  101.6 0.0 all-to-all-done
  101.6 50.7 %conditional.1 = (f32[1,4,256]{2,1,0:T(4,128)S(1)}, f32[1,4,256,128]{3,2,1,0:T(8,128)S(1)}) conditional(s32[]{:T(128)} %convert_element_type.17, () %tuple.16, (s32[8192]{0:T(1024)S(1)}, s32[]{:T(128)}, s32[256]{0:T(256)S(1)}, s32[8192]{0:T(1024)S(1)}, bf16[8192,1,128]{2,0,1:T(8,128)(2,1)}, /*index=5*/bf16[256,4,128]{2,1,0:T(4,128)(2,1)}, ...), branch_computations={%region_0.0_spmd, %region_1.4_spmd} | conditional | flops 4410309632 | bytes 114128952 | solution.py:66
  101.6 0.1 dynamic_slice.4
  101.7 5.6 %compare_and_fusion = pred[256,8192]{0,1:T(8,128)(4,1)S(1)} fusion(s32[256]{0:T(256)S(1)} %dynamic_slice.4, s32[256]{0:T(256)S(1)} %broadcast_add_fusion, s32[8192]{0:T(1024)S(1)} %get-tuple-element.59, s32[8192]{0:T(1024)S(1)} %get-tuple-element.56), kind=kLoop, calls=%fused_computation.8 | loop fusion | flops 6291456 | bytes 2164736 | tf_op jit(solution)/shard_map/cond/branch_1_fun/and | solution.py:48
  107.3 14.7 %fusion = (f32[4,256]{1,0:T(4,128)S(1)}, f32[8192,256,4]{1,0,2:T(8,128)}) fusion(pred[256,8192]{0,1:T(8,128)(4,1)S(1)} %compare_and_fusion, bf16[256,4,128]{2,1,0:T(4,128)(2,1)} %get-tuple-element.95, bf16[8192,1,128]{2,0,1:T(8,128)(2,1)} %get-tuple-element.60), kind=kOutput, calls=%fused_computation.2 | convolution fusion | flops 2172648448 | bytes 38014976 | tf_op jit(solution)/shard_map/cond/branch_1_fun/nhgd,khd->hgnk/dot_general | solution.py:45
  122.0 15.2 %fusion.9 = f32[1,4,256,128]{3,2,1,0:T(8,128)S(1)} fusion(bf16[8192,128,1]{1,0,2:T(8,128)(2,1)S(1)} %bitcast.48, f32[8192,256,4]{1,0,2:T(8,128)} %get-tuple-element.98, f32[4,256]{1,0:T(4,128)S(1)} %broadcast_maximum_fusion, pred[256,8192]{0,1:T(8,128)(4,1)S(1)} %compare_and_fusion), kind=kOutput, calls=%fused_computation.11 | convolution fusion | flops 2189426688 | bytes 38277120 | tf_op jit(solution)/shard_map/cond/branch_1_fun/hgnk,khd->hgnd/dot_general | solution.py:55
  137.3 15.0 %fusion.2 = f32[4,256]{1,0:T(4,128)S(1)} fusion(f32[8192,256,4]{1,0,2:T(8,128)} %get-tuple-element.98, f32[4,256]{1,0:T(4,128)S(1)} %broadcast_maximum_fusion, pred[256,8192]{0,1:T(8,128)(4,1)S(1)} %compare_and_fusion), kind=kLoop, calls=%fused_computation.4 | loop fusion | flops 41942016 | bytes 35659776 | tf_op jit(solution)/shard_map/cond/branch_1_fun/reduce_sum | solution.py:54
  152.3 0.2 fusion.16
  152.5 0.2 copy.18
  152.8 0.1 convert_element_type.20
  152.9 17.4 %all_to_all.21 = bf16[8,32,512]{2,1,0:T(8,128)(2,1)S(1)} all-to-all(bf16[8,32,512]{2,1,0:T(8,128)(2,1)S(1)} %convert_element_type.20), channel_id=1, replica_groups=mesh['ctx'=32,'head'=8] {'head'}, dimensions={0} | all-to-all | bytes 524288 | tf_op jit(solution)/shard_map/all_to_all | solution.py:84
  170.2 0.7 copy.21
  (4 shorter events, 0.0 us)
Async XLA Ops:
  6.5 95.0 %all-gather.3.cloned.1.call-start = ((), (), s32[]{:S(2)}) async-start(), calls=%async_computation.2 | async-start | bytes 2162688 | tf_op jit(solution)/shard_map/all_gather | solution.py:31
  9.9 91.7 %all-to-all-start = ((bf16[32,256,1,128]{3,1,2,0:T(8,128)(2,1)}), bf16[32,256,1,128]{3,1,2,0:T(8,128)(2,1)S(1)}, u32[]{:S(2)}, u32[]{:S(2)}) async-start(bf16[32,256,1,128]{3,1,2,0:T(8,128)(2,1)} %stack.2), calls=%async_computation | async-start | bytes 4194304 | tf_op jit(solution)/shard_map/all_to_all | solution.py:33
Sparse Core Ops, SparseCore 0:
  9.9 83.0 all-gather.2
